TPU v7x, 256 devices: a whole 4x4x8 slice. The times are simulated.
256 devices in a mesh: pb: 64 (over x, z, core), ka: 4 (over y).
Axes of the slice: x: 4, y: 4, z: 8, core: 2. Of those that a mesh axis runs over, the one named last changes fastest.
Arguments:
- valence: float32 [1664, 64, 1024], P('pb', 'ka'), may hold values from -6 to 6
- conduction: bfloat16 [1664, 196, 1024], P('pb', None, 'ka'), may hold values from -0.0024414062 to 0.0024414062
- screened: float32 [64, 1024, 1024], P('pb'), may hold values from -1 to 3, as said below
- momentum: int32 [1664, 1], P('pb'), may hold values from 0 to 63; in each aligned block of 26 rows (0 to 25, 26 to 51, ...) at most 2 rows name the same one
- kpairs: int32 [1664, 2], P('pb'), may hold values from 0 to 63
- kpoint_slot: int32 [64], replicated, may hold values from 0 to 63, each once
- trial_blocks: float32 [64, 14336], P('pb', 'ka'), may hold values from -6 to 6
Outputs:
- response: float32 [64, 14336], P('pb', 'ka')
Inputs may be any that keep to these rules, and one draw needn't show every extreme that they name: Among the k-pairs of one index of pb (rows i * 26 to (i + 1) * 26 - 1), at most 2 share a momentum transfer. `kpoint_slot`: each row number appears once. `screened`: each matrix is symmetric.
All inputs are finite; a program needn't handle non-finite values.
Results may differ from a plain program's by a relative error of at most 0.0003.
Values sent between devices are 32-bit elements; how exact they have to be, the bound alone decides.
No kernel may reach another device: no remote copies, remote signals or barrier semaphores. Data moves between devices by JAX's collectives and lax.ppermute only.
A program may use at most 128 MiB of HBM per device.

v0:
```python
import jax
import jax.numpy as jnp
from jax import lax
from jax.sharding import PartitionSpec as P

VB = 8
CB = 14


def local(valence, conduction, screened, momentum, kpairs, kpoint_slot, trial_blocks):
    highest = lax.Precision.HIGHEST
    pair_dev = valence.shape[0]
    owners = lax.axis_size("pb")
    capacity = max(2, 2 * pair_dev // owners)
    slot_count = owners * capacity
    target = momentum[:, 0]
    indices = jnp.arange(pair_dev, dtype=jnp.int32)
    earlier = (target[:, None] == target[None, :]) & (indices[None, :] < indices[:, None])
    position = target * capacity + jnp.sum(earlier.astype(jnp.int32), axis=1)
    matches = position[None, :] == jnp.arange(slot_count, dtype=jnp.int32)[:, None]
    source = jnp.sum(jnp.where(matches, indices[None, :], 0), axis=1)
    filled = jnp.any(matches, axis=1)
    outgoing = jnp.where(filled[:, None, None], jnp.take(valence, source, axis=0), 0.0)
    outgoing = outgoing.reshape(owners, capacity, valence.shape[1], valence.shape[2])
    matrix = screened[0]
    product = jnp.einsum(
        "scrg,gh->scrh",
        lax.all_to_all(outgoing, "pb", split_axis=0, concat_axis=0, tiled=True),
        matrix,
        precision=highest,
        preferred_element_type=jnp.float32,
    )
    returned = lax.all_to_all(
        lax.all_to_all(product, "pb", split_axis=0, concat_axis=0, tiled=True),
        "ka",
        split_axis=3,
        concat_axis=2,
        tiled=True,
    )
    by_slot = returned.reshape(slot_count, returned.shape[2], returned.shape[3])
    columns = jnp.take(by_slot, position, axis=0)
    conduct_wide = conduction.astype(jnp.float32)
    partial_kernel = jnp.einsum(
        "prg,pbg->prb", columns, conduct_wide, precision=highest, preferred_element_type=jnp.float32
    )
    kernel = lax.psum(partial_kernel, "ka")
    gathered = lax.all_gather(trial_blocks, "pb", axis=0, tiled=True)
    kpoint_count = gathered.shape[0]
    local_trials = gathered.shape[1] // (VB * CB)
    blocks = gathered.reshape(kpoint_count, local_trials, VB, CB)
    slot_near = jnp.take(kpoint_slot, kpairs[:, 0])
    slot_far = jnp.take(kpoint_slot, kpairs[:, 1])
    near_trials = jnp.take(blocks, slot_near, axis=0)
    far_trials = jnp.take(blocks, slot_far, axis=0)
    kernel_blocks = kernel.reshape(pair_dev, VB, VB, CB, CB)
    direct = jnp.einsum("pvwcd,pnwd->pnvc", kernel_blocks, far_trials, precision=highest)
    mirror = jnp.einsum("pvwcd,pnvc->pnwd", kernel_blocks, near_trials, precision=highest)
    kpoint_rows = jnp.arange(kpoint_count, dtype=jnp.int32)[:, None]
    onehot_near = (slot_near[None, :] == kpoint_rows).astype(jnp.float32)
    onehot_far = (slot_far[None, :] == kpoint_rows).astype(jnp.float32)
    summed = jnp.dot(
        onehot_near,
        direct.reshape(pair_dev, -1),
        precision=highest,
        preferred_element_type=jnp.float32,
    )
    summed = summed + jnp.dot(
        onehot_far,
        mirror.reshape(pair_dev, -1),
        precision=highest,
        preferred_element_type=jnp.float32,
    )
    return lax.psum_scatter(summed, "pb", scatter_dimension=0, tiled=True)


def solution(mesh):
    return jax.shard_map(
        local,
        mesh=mesh,
        in_specs=(
            P("pb", "ka", None),
            P("pb", None, "ka"),
            P("pb", None, None),
            P("pb", None),
            P("pb", None),
            P(),
            P("pb", "ka"),
        ),
        out_specs=P("pb", "ka"),
        check_vma=False,
    )
```

profile of v0, /device:TPU:8, one launch (start us, length us, event | category | flops | bytes accessed | tf_op | source)
XLA Modules:
  0.0 1163.5 jit_solution(17893508544063465319)
XLA Ops:
  6.5 0.0 copy-start
  6.5 1.0 convert_reduce_fusion
  7.5 0.7 multiply_add_fusion
  8.2 0.1 select_reduce_fusion
  8.3 0.1 fusion.16
  8.4 0.1 reduce_sum.27
  8.5 0.1 broadcast_in_dim.68
  8.7 5.8 gather_fusion
  14.5 4.0 select_select_fusion
  18.4 0.0 copy-start.5
  18.5 198.0 %all_to_all.25 = f32[64,2,16,1024]{3,2,1,0:T(8,128)S(1)} all-to-all(f32[64,2,16,1024]{3,2,1,0:T(8,128)S(1)} %select_select_fusion), channel_id=1, replica_groups=mesh['pb'=64,'ka'=4] {'pb'}, dimensions={0} | all-to-all | bytes 16777216 | tf_op jit(solution)/shard_map/all_to_all | solution.py:28
  216.4 0.0 copy-done.5
  216.4 27.7 %fusion = f32[64,2,16,1024]{3,2,1,0:T(8,128)S(1)} fusion(f32[64,2,16,1024]{3,2,1,0:T(8,128)S(1)} %all_to_all.25, f32[1,1024,1024]{2,1,0:T(8,128)S(1)} %copy-done.5), kind=kOutput, calls=%fused_computation.8 | convolution fusion | flops 25769803776 | bytes 20971520 | tf_op jit(solution)/shard_map/scrg,gh->scrh/dot_general | solution.py:26
  244.1 192.1 %all_to_all.26 = f32[64,2,16,1024]{3,2,1,0:T(8,128)} all-to-all(f32[64,2,16,1024]{3,2,1,0:T(8,128)S(1)} %fusion), channel_id=1, replica_groups=mesh['pb'=64,'ka'=4] {'pb'}, dimensions={0} | all-to-all | bytes 16777216 | tf_op jit(solution)/shard_map/all_to_all | solution.py:34
  436.2 16.3 %copy.61 = f32[64,2,16,1024]{0,2,1,3:T(8,128)} copy(f32[64,2,16,1024]{3,2,1,0:T(8,128)} %all_to_all.26) | data formatting | bytes 16777216 | tf_op jit(solution)/shard_map/all_to_all | solution.py:34
  452.5 14.3 %reshape.142 = f32[4,1,524288]{2,1,0:T(1,128)} reshape(f32[1024,2,16,64]{3,2,1,0:T(8,128)} %bitcast.68) | data formatting | bytes 16777216
  466.8 0.0 copy-start.4
  466.8 6.2 all-to-all-start.2
  473.0 0.0 all-reduce.4.cloned.1.call-start
  473.0 0.0 copy-done.4
  473.0 92.9 %all-to-all-done.2 = f32[4,1,524288]{2,1,0:T(1,128)} async-done(((f32[4,1,524288]{2,1,0:T(1,128)}), f32[4,1,524288]{2,1,0:T(1,128)}, u32[]{:S(2)}, u32[]{:S(2)}) %all-to-all-start.2) | async-done | bytes 8388640 | tf_op jit(solution)/shard_map/all_to_all | solution.py:33
  566.0 0.5 broadcast.181
  566.5 30.1 %reduce = f32[4,524288]{1,0:T(4,128)} reduce(f32[4,1,524288]{2,1,0:T(1,128)} %all-to-all-done.2, f32[]{:T(128)} %broadcast.181), dimensions={1}, to_apply=%all_to_all.19.reduce_sub_computation | reduce | bytes 16777220 | tf_op jit(solution)/shard_map/all_to_all | solution.py:33
  596.6 16.8 %reshape.143 = f32[1024,2,16,64]{3,2,1,0:T(8,128)} reshape(f32[4,524288]{1,0:T(4,128)} %reduce) | data formatting | bytes 16777216
  613.4 14.4 %copy.75 = f32[64,2,16,4,256]{4,3,2,1,0:T(4,128)} copy(f32[64,2,16,4,256]{0,2,1,4,3:T(8,128)} %bitcast.69) | data formatting | bytes 16777216 | tf_op jit(solution)/shard_map/all_to_all | solution.py:33
  627.8 8.6 copy.63
  636.4 5.3 gather_fusion.1
  641.7 0.0 copy-done
  641.7 5.3 fusion.2
  647.0 5.8 copy.64
  652.8 14.5 %copy.65 = f32[26,8,8,14,14]{3,2,4,1,0:T(8,128)} copy(f32[26,8,8,14,14]{0,2,1,4,3:T(8,128)} %bitcast.72) | data formatting | bytes 2609152 | tf_op jit(solution)/shard_map/reshape | solution.py:55
  667.3 0.0 copy-start.3
  667.3 0.0 copy-start.1
  667.3 0.0 copy-start.2
  667.3 0.0 all-reduce.4.cloned.1.call-update
  667.3 0.0 all-reduce.6.cloned.1.call-start
  667.4 0.6 copy-done.3
  668.0 0.0 copy-done.1
  668.0 0.7 gather_fusion.3
  668.7 0.7 gather_fusion.2
  669.4 0.0 copy-done.2
  669.4 52.6 %all-gather = f32[64,1,3584]{2,1,0:T(1,128)} all-gather(f32[1,1,3584]{2,1,0:T(1,128)S(1)} %bitcast.74), channel_id=1, replica_groups=mesh['pb'=64,'ka'=4] {'pb'}, dimensions={0}, use_global_device_ids=true | all-gather | bytes 931840 | tf_op jit(solution)/shard_map/all_gather | solution.py:47
  722.0 4.1 copy.59
  726.1 2.7 reshape.68
  728.7 5.5 copy.60
  734.2 3.9 gather_fusion.5
  738.1 3.8 gather_fusion.4
  741.9 142.4 %all-reduce.4.cloned.1.call-done = f32[26,8,8,14,14]{3,2,4,1,0:T(8,128)} async-done(((f32[26,8,8,14,14]{3,2,4,1,0:T(8,128)}), f32[26,8,8,14,14]{3,2,4,1,0:T(8,128)}) %all-reduce.4.cloned.1.call-update) | async-done | bytes 1304592 | tf_op jit(solution)/shard_map/psum | solution.py:46
  884.3 16.3 %copy.68 = f32[26,8,8,14,14]{4,1,3,2,0:T(8,128)} copy(f32[26,8,8,14,14]{3,2,4,1,0:T(8,128)} %all-reduce.4.cloned.1.call-done) | data formatting | bytes 2609152 | tf_op jit(solution)/shard_map/psum | solution.py:46
  900.7 22.8 %convolution_bitcast_fusion = f32[26,32,8,14]{1,3,2,0:T(8,128)} fusion(f32[26,8,8,14,14]{4,1,3,2,0:T(8,128)} %copy.68, f32[26,32,8,14]{1,2,3,0:T(8,128)} %gather_fusion.5, pred[26]{0:T(512)(128)(4,1)S(1)} %get-tuple-element.6), kind=kOutput, calls=%fused_computation.12 | convolution fusion | flops 125332480 | bytes 2050074 | tf_op jit(solution)/shard_map/pvwcd,pnvc->pnwd/dot_general | solution.py:57
  923.5 3.7 copy.69
  927.2 4.0 reshape.72
  931.2 23.0 %convolution_bitcast_fusion.1 = f32[26,32,8,14]{1,3,2,0:T(8,128)} fusion(f32[26,8,8,14,14]{3,2,4,1,0:T(8,128)} %all-reduce.4.cloned.1.call-done, f32[26,32,8,14]{1,2,3,0:T(8,128)} %gather_fusion.4, pred[26]{0:T(512)(128)(4,1)S(1)} %get-tuple-element.13), kind=kOutput, calls=%fused_computation.13 | convolution fusion | flops 125332480 | bytes 2050074 | tf_op jit(solution)/shard_map/pvwcd,pnwd->pnvc/dot_general | solution.py:56
  954.2 3.7 copy.66
  957.9 0.0 copy-start.6
  957.9 4.6 reshape.71
  962.5 1.5 fusion.14
  964.0 1.5 convolution_add_fusion
  965.5 0.0 all-reduce.6.cloned.1.call-update
  965.5 0.0 copy-done.6
  965.5 0.7 dynamic-slice
  966.2 188.0 %all-reduce.6.cloned.1.call-done = f32[64,3584]{1,0:T(8,128)} async-done(((f32[64,3584]{1,0:T(8,128)}), f32[64,3584]{1,0:T(8,128)}) %all-reduce.6.cloned.1.call-update) | async-done | bytes 917520
  1154.2 2.2 constant_dynamic-slice_fusion
  (12 shorter events, 0.1 us)
Async XLA Ops:
  6.5 635.1 %copy-start = (bf16[26,196,256]{2,1,0:T(8,128)(2,1)S(1)}, bf16[26,196,256]{2,1,0:T(8,128)(2,1)}, u32[]{:S(2)}) copy-start(bf16[26,196,256]{2,1,0:T(8,128)(2,1)} %param.12) | copy-start | bytes 7827460
  18.4 198.0 %copy-start.5 = (f32[1,1024,1024]{2,1,0:T(8,128)S(1)}, f32[1,1024,1024]{2,1,0:T(8,128)}, u32[]{:S(2)}) copy-start(f32[1,1024,1024]{2,1,0:T(8,128)} %param.13) | copy-start | bytes 12582916
  466.8 6.2 copy-start.4
  466.8 99.1 %all-to-all-start.2 = ((f32[4,1,524288]{2,1,0:T(1,128)}), f32[4,1,524288]{2,1,0:T(1,128)}, u32[]{:S(2)}, u32[]{:S(2)}) async-start(f32[4,1,524288]{2,1,0:T(1,128)} %reshape.142), calls=%async_computation.2 | async-start | bytes 16777216 | tf_op jit(solution)/shard_map/all_to_all | solution.py:33
  473.0 411.3 %all-reduce.4.cloned.1.call-start = ((), (), s32[]{:S(2)}) async-start(), calls=%async_computation.3 | async-start | bytes 23855104 | tf_op jit(solution)/shard_map/psum | solution.py:46
  667.3 0.7 copy-start.3
  667.3 0.7 copy-start.1
  667.3 2.1 copy-start.2
  667.3 486.9 %all-reduce.6.cloned.1.call-start = ((), (), s32[]{:S(2)}) async-start(), calls=%async_computation.4 | async-start | bytes 1835008
  957.9 7.6 copy-start.6
Sparse Core Ops, SparseCore 0:
  667.4 216.8 all-reduce.3
  965.7 188.5 all-reduce.5
where the time goes:
time: 1170 us; the launch traced here: 1160 us
  blocking collectives  443 us (38%)
  waiting for transfers between devices  423 us (36%)
  local copies, waits for them, and re-layouts  160 us (14%)
  matrix products  81.8 us (7%)
  other arithmetic  36 us (3%)
  between operations  13.8 us (1%)
    all_to_all x1, blocking collectives, local(): lax.all_to_all(outgoing, 'pb', split_axis=0, concat_axis=0, tiled=True)  198 us
    all_to_all x1, blocking collectives, local(): lax.all_to_all(product, 'pb', split_axis=0, concat_axis=0, tiled=True)  192 us
    unnamed x3, waiting for transfers between devices  188 us
    psum x1, waiting for transfers between devices, local(): kernel = lax.psum(partial_kernel, 'ka')  142 us
    all_to_all x1, waiting for transfers between devices, local(): lax.all_to_all(lax.all_to_all(product, 'pb', split_axis=0, concat_axis=0,...  92.9 us
    all_gather x1, blocking collectives, local(): gathered = lax.all_gather(trial_blocks, 'pb', axis=0, tiled=True)  52.6 us
    unnamed x18, local copies, waits for them, and re-layouts  34.6 us
    all_to_all x1, other arithmetic, local(): lax.all_to_all(lax.all_to_all(product, 'pb', split_axis=0, concat_axis=0,...  30.1 us
  transfers between devices with their start and end apart: 3, of which 3 were waited for; matrix products, arithmetic and copies ran while one was open for 2% of the time, Pallas kernels for 0%

commit v1 on v0

--- a/solution.py
+++ b/solution.py
@@ -43,7 +43,7 @@
     partial_kernel = jnp.einsum(
         "prg,pbg->prb", columns, conduct_wide, precision=highest, preferred_element_type=jnp.float32
     )
-    kernel = lax.psum(partial_kernel, "ka")
+    kernel = jnp.sum(lax.all_gather(partial_kernel, "ka"), axis=0)
     gathered = lax.all_gather(trial_blocks, "pb", axis=0, tiled=True)
     kpoint_count = gathered.shape[0]
     local_trials = gathered.shape[1] // (VB * CB)

time: 1170 us -> 1040 us (0.89)
  waiting for transfers between devices: 423 us -> 277 us
    psum x1 -> x0, waiting for transfers between devices: 142 us -> none  [local(): kernel = lax.psum(partial_kernel, 'ka')]
    psum x1 -> x0, local copies, waits for them, and re-layouts: 16.3 us -> none  [local(): kernel = lax.psum(partial_kernel, 'ka')]
    reshape x1 -> x2, local copies, waits for them, and re-layouts: 14.5 us -> 29.1 us  [local(): kernel_blocks = kernel.reshape(pair_dev, VB, VB, CB, CB)]
  transfers between devices with their start and end apart: 3 -> 3, of which waited for: 3 -> 2; matrix products, arithmetic and copies ran while one was open for 2% -> 2% of each run, Pallas kernels for 0% -> 0%
where the time goes in v1:
time: 1040 us; the launch traced here: 1030 us
  blocking collectives  442 us (42%)
  waiting for transfers between devices  277 us (27%)
  local copies, waits for them, and re-layouts  165 us (16%)
  matrix products  83.2 us (8%)
  other arithmetic  41.1 us (4%)
  between operations  14 us (1%)
    all_to_all x1, blocking collectives, local(): lax.all_to_all(outgoing, 'pb', split_axis=0, concat_axis=0, tiled=True)  198 us
    all_to_all x1, blocking collectives, local(): lax.all_to_all(product, 'pb', split_axis=0, concat_axis=0, tiled=True)  192 us
    unnamed x3, waiting for transfers between devices  184 us
    all_to_all x1, waiting for transfers between devices, local(): lax.all_to_all(lax.all_to_all(product, 'pb', split_axis=0, concat_axis=0,...  92.9 us
    all_gather x1, blocking collectives, local(): gathered = lax.all_gather(trial_blocks, 'pb', axis=0, tiled=True)  52.3 us
    unnamed x18, local copies, waits for them, and re-layouts  33.9 us
    all_to_all x3, local copies, waits for them, and re-layouts, local(): lax.all_to_all(lax.all_to_all(product, 'pb', split_axis=0, concat_axis=0,...  32.2 us
    all_to_all x1, other arithmetic, local(): lax.all_to_all(lax.all_to_all(product, 'pb', split_axis=0, concat_axis=0,...  30.1 us
  transfers between devices with their start and end apart: 3, of which 2 were waited for; matrix products, arithmetic and copies ran while one was open for 2% of the time, Pallas kernels for 0%

profile of v1, /device:TPU:8, one launch (start us, length us, event | category | flops | bytes accessed | tf_op | source)
XLA Modules:
  0.0 1028.9 jit_solution(14765611050665016095)
XLA Ops:
  6.5 0.0 copy-start
  6.5 1.0 convert_reduce_fusion
  7.5 0.7 multiply_add_fusion
  8.2 0.1 select_reduce_fusion
  8.3 0.1 reduce_sum.36
  8.4 0.1 fusion.16
  8.6 0.1 broadcast_in_dim.68
  8.7 5.8 gather_fusion
  14.5 4.0 select_select_fusion
  18.4 0.0 copy-start.5
  18.5 198.0 %all_to_all.25 = f32[64,2,16,1024]{3,2,1,0:T(8,128)S(1)} all-to-all(f32[64,2,16,1024]{3,2,1,0:T(8,128)S(1)} %select_select_fusion), channel_id=1, replica_groups=mesh['pb'=64,'ka'=4] {'pb'}, dimensions={0} | all-to-all | bytes 16777216 | tf_op jit(solution)/shard_map/all_to_all | solution.py:28
  216.4 0.0 copy-done.5
  216.4 27.7 %fusion = f32[64,2,16,1024]{3,2,1,0:T(8,128)S(1)} fusion(f32[64,2,16,1024]{3,2,1,0:T(8,128)S(1)} %all_to_all.25, f32[1,1024,1024]{2,1,0:T(8,128)S(1)} %copy-done.5), kind=kOutput, calls=%fused_computation.8 | convolution fusion | flops 25769803776 | bytes 20971520 | tf_op jit(solution)/shard_map/scrg,gh->scrh/dot_general | solution.py:26
  244.1 192.2 %all_to_all.26 = f32[64,2,16,1024]{3,2,1,0:T(8,128)} all-to-all(f32[64,2,16,1024]{3,2,1,0:T(8,128)S(1)} %fusion), channel_id=1, replica_groups=mesh['pb'=64,'ka'=4] {'pb'}, dimensions={0} | all-to-all | bytes 16777216 | tf_op jit(solution)/shard_map/all_to_all | solution.py:34
  436.3 16.3 %copy.59 = f32[64,2,16,1024]{0,2,1,3:T(8,128)} copy(f32[64,2,16,1024]{3,2,1,0:T(8,128)} %all_to_all.26) | data formatting | bytes 16777216 | tf_op jit(solution)/shard_map/all_to_all | solution.py:34
  452.6 14.3 %reshape.143 = f32[4,1,524288]{2,1,0:T(1,128)} reshape(f32[1024,2,16,64]{3,2,1,0:T(8,128)} %bitcast.69) | data formatting | bytes 16777216
  466.9 0.0 copy-start.4
  466.9 6.2 all-to-all-start.2
  473.1 0.0 all-gather.4.cloned.1.call-start
  473.1 0.0 copy-done.4
  473.1 92.9 %all-to-all-done.2 = f32[4,1,524288]{2,1,0:T(1,128)} async-done(((f32[4,1,524288]{2,1,0:T(1,128)}), f32[4,1,524288]{2,1,0:T(1,128)}, u32[]{:S(2)}, u32[]{:S(2)}) %all-to-all-start.2) | async-done | bytes 8388640 | tf_op jit(solution)/shard_map/all_to_all | solution.py:33
  566.0 0.5 broadcast.181
  566.6 30.1 %reduce = f32[4,524288]{1,0:T(4,128)} reduce(f32[4,1,524288]{2,1,0:T(1,128)} %all-to-all-done.2, f32[]{:T(128)} %broadcast.181), dimensions={1}, to_apply=%all_to_all.19.reduce_sub_computation | reduce | bytes 16777220 | tf_op jit(solution)/shard_map/all_to_all | solution.py:33
  596.7 16.8 %reshape.144 = f32[1024,2,16,64]{3,2,1,0:T(8,128)} reshape(f32[4,524288]{1,0:T(4,128)} %reduce) | data formatting | bytes 16777216
  613.5 23.1 %copy.73 = f32[64,2,16,4,256]{4,3,2,1,0:T(4,128)} copy(f32[64,2,16,4,256]{0,2,1,4,3:T(8,128)} %bitcast.70) | data formatting | bytes 16777216 | tf_op jit(solution)/shard_map/all_to_all | solution.py:33
  636.5 8.6 copy.61
  645.1 5.3 gather_fusion.1
  650.4 0.0 copy-done
  650.4 0.0 copy-start.3
  650.4 0.0 copy-start.1
  650.4 0.0 copy-start.2
  650.4 5.4 fusion.2
  655.8 0.0 all-gather.4.cloned.1.call-update
  655.8 0.0 all-reduce.3.cloned.1.call-start
  655.9 0.0 copy-done.3
  655.9 0.0 copy-done.1
  655.9 0.7 gather_fusion.2
  656.6 0.7 gather_fusion.3
  657.3 0.0 copy-done.2
  657.3 52.3 %all-gather.1 = f32[64,1,3584]{2,1,0:T(1,128)} all-gather(f32[1,1,3584]{2,1,0:T(1,128)S(1)} %bitcast.77), channel_id=1, replica_groups=mesh['pb'=64,'ka'=4] {'pb'}, dimensions={0}, use_global_device_ids=true | all-gather | bytes 931840 | tf_op jit(solution)/shard_map/all_gather | solution.py:47
  709.7 3.9 copy.57
  713.6 2.6 reshape.68
  716.2 5.5 copy.58
  721.7 3.8 gather_fusion.4
  725.6 3.8 gather_fusion.5
  729.4 0.0 all-gather.4.cloned.1.call-done
  729.4 5.1 reduce_sum.38
  734.5 5.7 copy.62
  740.2 14.5 %copy.63 = f32[26,8,8,14,14]{3,2,4,1,0:T(8,128)} copy(f32[26,8,8,14,14]{0,2,1,4,3:T(8,128)} %bitcast.71) | data formatting | bytes 2609152 | tf_op jit(solution)/shard_map/reshape | solution.py:55
  754.7 14.6 %copy.66 = f32[26,8,8,14,14]{4,1,3,2,0:T(8,128)} copy(f32[26,8,8,14,14]{0,2,1,4,3:T(8,128)} %bitcast.72) | data formatting | bytes 2609152 | tf_op jit(solution)/shard_map/reshape | solution.py:55
  769.3 23.0 %convolution_bitcast_fusion.1 = f32[26,32,8,14]{1,3,2,0:T(8,128)} fusion(f32[26,8,8,14,14]{3,2,4,1,0:T(8,128)} %copy.63, f32[26,32,8,14]{1,2,3,0:T(8,128)} %gather_fusion.4, pred[26]{0:T(512)(128)(4,1)S(1)} %get-tuple-element.13), kind=kOutput, calls=%fused_computation.13 | convolution fusion | flops 125332480 | bytes 2050074 | tf_op jit(solution)/shard_map/pvwcd,pnwd->pnvc/dot_general | solution.py:56
  792.3 3.7 copy.64
  796.0 4.0 reshape.71
  800.0 1.4 fusion.14
  801.5 23.0 %convolution_bitcast_fusion = f32[26,32,8,14]{1,3,2,0:T(8,128)} fusion(f32[26,8,8,14,14]{4,1,3,2,0:T(8,128)} %copy.66, f32[26,32,8,14]{1,2,3,0:T(8,128)} %gather_fusion.5, pred[26]{0:T(512)(128)(4,1)S(1)} %get-tuple-element.6), kind=kOutput, calls=%fused_computation.12 | convolution fusion | flops 125332480 | bytes 2050074 | tf_op jit(solution)/shard_map/pvwcd,pnvc->pnwd/dot_general | solution.py:57
  824.5 3.7 copy.67
  828.2 0.0 copy-start.6
  828.2 4.0 reshape.72
  832.2 2.6 convolution_add_fusion
  834.8 0.0 all-reduce.3.cloned.1.call-update
  834.8 0.0 copy-done.6
  834.8 0.6 dynamic-slice
  835.5 184.0 %all-reduce.3.cloned.1.call-done = f32[64,3584]{1,0:T(8,128)} async-done(((f32[64,3584]{1,0:T(8,128)}), f32[64,3584]{1,0:T(8,128)}) %all-reduce.3.cloned.1.call-update) | async-done | bytes 917520
  1019.5 2.1 constant_dynamic-slice_fusion
  (12 shorter events, 0.1 us)
Async XLA Ops:
  6.5 643.9 %copy-start = (bf16[26,196,256]{2,1,0:T(8,128)(2,1)S(1)}, bf16[26,196,256]{2,1,0:T(8,128)(2,1)}, u32[]{:S(2)}) copy-start(bf16[26,196,256]{2,1,0:T(8,128)(2,1)} %param.12) | copy-start | bytes 7827460
  18.4 198.0 %copy-start.5 = (f32[1,1024,1024]{2,1,0:T(8,128)S(1)}, f32[1,1024,1024]{2,1,0:T(8,128)}, u32[]{:S(2)}) copy-start(f32[1,1024,1024]{2,1,0:T(8,128)} %param.13) | copy-start | bytes 12582916
  466.9 6.2 copy-start.4
  466.9 99.1 %all-to-all-start.2 = ((f32[4,1,524288]{2,1,0:T(1,128)}), f32[4,1,524288]{2,1,0:T(1,128)}, u32[]{:S(2)}, u32[]{:S(2)}) async-start(f32[4,1,524288]{2,1,0:T(1,128)} %reshape.143), calls=%async_computation.2 | async-start | bytes 16777216 | tf_op jit(solution)/shard_map/all_to_all | solution.py:33
  473.1 256.3 %all-gather.4.cloned.1.call-start = ((), (), s32[]{:S(2)}) async-start(), calls=%async_computation.3 | async-start | bytes 8519680 | tf_op jit(solution)/shard_map/all_gather | solution.py:46
  650.4 5.5 copy-start.3
  650.4 5.5 copy-start.1
  650.4 6.9 copy-start.2
  655.8 363.7 %all-reduce.3.cloned.1.call-start = ((), (), s32[]{:S(2)}) async-start(), calls=%async_computation.4 | async-start | bytes 1835008
  828.2 6.6 copy-start.6
Sparse Core Ops, SparseCore 0:
  655.9 67.7 all-gather.3
  834.9 184.5 all-reduce.2
